TPU v7x, 128 devices: a whole 4x4x4 slice. The times are simulated.
128 devices in a mesh: dp: 4 (over y), label: 32 (over z, x, core).
Axes of the slice: x: 4, y: 4, z: 4, core: 2. Of those that a mesh axis runs over, the one named last changes fastest.
Arguments:
- queries: bfloat16 [32768, 768], P(('dp', 'label')), may hold values from -6 to 6
- weights: bfloat16 [32, 4096, 768], P('label'), as said below
- beam: int32 [256, 4], P(('dp', 'label')), may hold values from -1 to 31, as said below
- positives: int32 [32768], P(('dp', 'label')), may hold values from 0 to 131071, as said below
- owner: int32 [32], replicated, may hold values from 0 to 31, each once
Outputs:
- loss: float32 [32768], P(('dp', 'label'))
- grad_queries: float32 [32768, 768], P(('dp', 'label'))
- grad_weights: float32 [32, 4096, 768], P('label', 'dp')
Inputs may be any that keep to these rules, and one draw needn't show every extreme that they name: `beam`: each row lists 3 or 4 distinct block ids, then -1 entries. The query blocks of one device list pairwise different ids. Within each aligned group of 64 rows (the query blocks of one dp index) no id stands in more than 8 rows, and some id stands in exactly 8 rows. `positives`: the positive label id of query n lies in a block listed in the beam row of n // 128. `weights`: entries lie within -18 / sqrt(768) to 18 / sqrt(768).
All inputs are finite; a program needn't handle non-finite values.
Results may differ from a plain program's by a relative error of at most 0.013.
Values may be sent and summed in bfloat16 or wider, within the bound.
No kernel may reach another device: no remote copies, remote signals or barrier semaphores. Data moves between devices by JAX's collectives and lax.ppermute only.
A program may use at most 128 MiB of HBM per device.

v0:
```python
import jax
import jax.numpy as jnp
from jax import lax
from jax.sharding import PartitionSpec as P


def per_device(queries, weights, beam, positives, owner):
    label_size = lax.axis_size("label")
    my_label = lax.axis_index("label")
    home_blocks = beam.shape[0]
    beam_width = beam.shape[1]
    block_rows = queries.shape[0] // home_blocks
    features = queries.shape[1]
    block_size = weights.shape[1]
    block_total = owner.shape[0]
    slot_count = home_blocks * beam_width
    block_ids = jnp.arange(block_total, dtype=jnp.int32)
    device_ids = jnp.arange(label_size, dtype=jnp.int32)
    home_range = jnp.arange(home_blocks, dtype=jnp.int32)

    def destinations(block_list):
        matches = block_list[..., None] == block_ids
        found = jnp.sum(jnp.where(matches, owner, 0), axis=-1)
        return jnp.where(block_list >= 0, found, -1)

    home_dest = destinations(beam)
    home_hit = jnp.any(home_dest[:, :, None] == device_ids[None, None, :], axis=1)
    home_pick = jnp.sum(jnp.where(home_hit, home_range[:, None], 0), axis=0)
    home_used = jnp.any(home_hit, axis=0)
    gathered_lists, gathered_wanted = (
        lax.all_gather(beam, "label", axis=0, tiled=True),
        lax.all_gather(positives, "label", axis=0, tiled=True),
    )
    owner_dest = destinations(gathered_lists)
    owner_hit = jnp.any(owner_dest == my_label, axis=1).reshape(label_size, home_blocks)
    touched = jnp.any(owner_hit, axis=1)
    source_pick = jnp.sum(jnp.where(owner_hit, home_range[None, :], 0), axis=1)
    ranking = jnp.cumsum(touched.astype(jnp.int32)) - 1
    slot_ids = jnp.arange(slot_count, dtype=jnp.int32)
    source = jnp.sum(
        jnp.where(
            touched[None, :] & (ranking[None, :] == slot_ids[:, None]), device_ids[None, :], 0
        ),
        axis=1,
    )
    active = slot_ids < jnp.sum(touched.astype(jnp.int32))
    chosen = source * home_blocks + source_pick[source]
    my_block = jnp.sum(jnp.where(owner == my_label, block_ids, 0))
    everyone = lax.all_gather(queries, "label", axis=0, tiled=True)
    routed = everyone.reshape(label_size * home_blocks, block_rows, features)[chosen]
    flat_rows = routed.reshape(slot_count * block_rows, features)
    ranker = weights[0]
    scores = lax.dot_general(
        flat_rows, ranker, (((1,), (1,)), ((), ())), preferred_element_type=jnp.float32
    )
    highest = jnp.max(scores, axis=1)
    exp_total = jnp.sum(jnp.exp(scores - highest[:, None]), axis=1)
    wanted_rows = gathered_wanted.reshape(label_size * home_blocks, block_rows)[chosen].reshape(-1)
    in_block = wanted_rows // block_size == my_block
    target = (
        jnp.arange(block_size, dtype=jnp.int32)[None, :] == (wanted_rows % block_size)[:, None]
    ) & in_block[:, None]
    picked = jnp.sum(jnp.where(target, scores, 0.0), axis=1)

    def to_sources(values):
        keep = active.reshape((slot_count,) + (1,) * (values.ndim - 1))
        masked = jnp.where(keep, values, jnp.zeros((), values.dtype))
        return jnp.zeros((label_size,) + values.shape[1:], values.dtype).at[source].add(masked)

    got_high, got_total, got_pick = (
        lax.all_to_all(
            to_sources(highest.reshape(slot_count, block_rows)),
            "label",
            split_axis=0,
            concat_axis=0,
            tiled=True,
        ),
        lax.all_to_all(
            to_sources(exp_total.reshape(slot_count, block_rows)),
            "label",
            split_axis=0,
            concat_axis=0,
            tiled=True,
        ),
        lax.all_to_all(
            to_sources(picked.reshape(slot_count, block_rows)),
            "label",
            split_axis=0,
            concat_axis=0,
            tiled=True,
        ),
    )
    hit_mask = home_hit[:, :, None]
    biggest = jnp.max(jnp.where(hit_mask, got_high[None], -jnp.inf), axis=1)
    shifted = jnp.exp(jnp.where(hit_mask, got_high[None] - biggest[:, None, :], 0.0))
    summed = jnp.sum(jnp.where(hit_mask, got_total[None] * shifted, 0.0), axis=1)
    normal = biggest + jnp.log(summed)
    positive = jnp.sum(jnp.where(hit_mask, got_pick[None], 0.0), axis=1)
    loss = (normal - positive).reshape(-1)
    sendback = jnp.where(home_used[:, None], normal[home_pick], 0.0)
    normal_in = lax.all_to_all(sendback, "label", split_axis=0, concat_axis=0, tiled=True)
    normal_rows = normal_in[source].reshape(-1)
    active_rows = jnp.repeat(active, block_rows)
    slope = jnp.where(
        active_rows[:, None],
        jnp.exp(scores - normal_rows[:, None]) - target.astype(jnp.float32),
        0.0,
    ).astype(jnp.bfloat16)
    partial_rows = (
        jnp.dot(slope, ranker, preferred_element_type=jnp.float32)
        .astype(jnp.bfloat16)
        .reshape(slot_count, block_rows, features)
    )
    keep = active[:, None, None]
    dense = (
        jnp.zeros((label_size * home_blocks, block_rows, features), jnp.bfloat16)
        .at[chosen]
        .add(jnp.where(keep, partial_rows, jnp.zeros((), jnp.bfloat16)))
    )
    grad_queries = lax.psum_scatter(
        dense.reshape(label_size * home_blocks * block_rows, features),
        "label",
        scatter_dimension=0,
        tiled=True,
    ).astype(jnp.float32)
    grad_table = lax.psum_scatter(
        lax.dot_general(
            slope, flat_rows, (((0,), (0,)), ((), ())), preferred_element_type=jnp.float32
        ).astype(jnp.bfloat16),
        "dp",
        scatter_dimension=0,
        tiled=True,
    ).astype(jnp.float32)
    return (loss, grad_queries, grad_table[None])


def solution(mesh):
    placed = (
        P(("dp", "label"), None),
        P("label", None, None),
        P(("dp", "label"), None),
        P(("dp", "label")),
        P(),
    )
    return jax.shard_map(
        per_device,
        mesh=mesh,
        in_specs=placed,
        out_specs=(P(("dp", "label")), P(("dp", "label"), None), P("label", "dp", None)),
        check_vma=False,
    )
```

profile of v0, /device:TPU:2, one launch (start us, length us, event | category | flops | bytes accessed | tf_op | source)
XLA Modules:
  0.0 348.4 jit_solution(12113283157434922044)
XLA Ops:
  7.2 0.7 all-gather.4.cloned.1.call-update
  7.9 25.2 %all-gather = s32[32,2,4]{2,1,0:T(2,128)S(1)} all-gather(s32[1,2,4]{2,1,0:T(2,128)} %bitcast.110), channel_id=1, replica_groups=mesh['dp'=4,'label'=32] {'label'}, dimensions={0}, use_global_device_ids=true | all-gather | bytes 1056 | tf_op jit(solution)/shard_map/all_gather | solution.py:31
  33.2 0.8 select_reduce_fusion.1
  33.9 0.1 reshape.233
  34.1 0.1 reduce_or.38
  34.3 0.1 add_reduce_fusion
  34.4 0.1 select_reduce_fusion.6
  34.6 0.1 select_reduce_fusion.5
  34.7 0.6 gather_fusion
  35.4 21.9 %all-gather.1 = s32[32,1,256]{2,1,0:T(1,128)S(1)} all-gather(s32[1,1,256]{2,1,0:T(1,128)} %bitcast.111), channel_id=1, replica_groups=mesh['dp'=4,'label'=32] {'label'}, dimensions={0}, use_global_device_ids=true | all-gather | bytes 33792 | tf_op jit(solution)/shard_map/all_gather | solution.py:32
  57.3 0.6 gather_fusion.2
  57.9 0.6 convert_reduce_fusion
  58.5 0.7 iota_compare_fusion.5
  59.2 1.3 fusion.28
  60.5 0.9 select_reduce_fusion.7
  61.4 0.7 compare_select_fusion.4
  62.2 0.7 fusion.14
  62.8 12.9 %all-gather.4.cloned.1.call-done = bf16[8192,768]{1,0:T(8,128)(2,1)} async-done(((bf16[256,768]{1,0:T(8,128)(2,1)}), bf16[8192,768]{1,0:T(8,128)(2,1)}) %all-gather.4.cloned.1.call-update) | async-done | bytes 12582928 | tf_op jit(solution)/shard_map/all_gather | solution.py:49
  75.8 5.2 %gather_fusion.1 = bf16[8,128,768]{2,1,0:T(8,128)(2,1)S(1)} fusion(bf16[64,128,768]{2,1,0:T(8,128)(2,1)} %bitcast.101, s32[1024]{0:T(1024)S(1)} %pad_clamp_fusion.1), kind=kCustom, calls=%fused_computation.1 | custom fusion | bytes 3145760 | tf_op jit(solution)/shard_map/gather | solution.py:50
  81.0 9.0 %fusion.32 = (f32[1024]{0:T(1024)S(1)}, f32[1024,4096]{1,0:T(8,128)S(1)}) fusion(bf16[1024,768]{1,0:T(8,128)(2,1)S(1)} %bitcast.98, bf16[1,4096,768]{2,1,0:T(8,128)(2,1)} %param.6), kind=kOutput, calls=%fused_computation.87 | convolution fusion | flops 6446644224 | bytes 24645632 | tf_op jit(solution)/shard_map/dot_general | solution.py:53
  90.0 8.0 %select_reduce_fusion = (f32[1024]{0:T(1024)S(1)}, f32[1024]{0:T(1024)S(1)}) fusion(f32[1024,4096]{1,0:T(8,128)S(1)} %get-tuple-element.12, s32[1024]{0:T(1024)S(1)} %add_select_fusion.1, pred[1024]{0:T(1024)(128)(4,1)S(1)} %fusion.14, f32[1024]{0:T(1024)S(1)} %get-tuple-element.11), kind=kLoop, calls=%fused_computation.10 | loop fusion | flops 25163776 | bytes 16794624 | tf_op jit(solution)/shard_map/reduce_sum | solution.py:63
  98.0 1.2 scatter_custom_fusion.1
  99.3 5.7 %all-to-all-start.1 = ((f32[32,1,128]{2,1,0:T(1,128)}), f32[32,1,128]{2,1,0:T(1,128)S(1)}, u32[]{:S(2)}, u32[]{:S(2)}) async-start(f32[32,1,128]{2,1,0:T(1,128)} %bitcast.15), calls=%async_computation.1 | async-start | bytes 32768 | tf_op jit(solution)/shard_map/all_to_all | solution.py:78
  105.0 1.2 scatter_custom_fusion
  106.3 4.8 %all-to-all-done.1 = f32[32,1,128]{2,1,0:T(1,128)S(1)} async-done(((f32[32,1,128]{2,1,0:T(1,128)}), f32[32,1,128]{2,1,0:T(1,128)S(1)}, u32[]{:S(2)}, u32[]{:S(2)}) %all-to-all-start.1) | async-done | bytes 16416 | tf_op jit(solution)/shard_map/all_to_all | solution.py:78
  111.1 4.9 %all-to-all-start = ((f32[32,1,128]{2,1,0:T(1,128)}), f32[32,1,128]{2,1,0:T(1,128)S(1)}, u32[]{:S(2)}, u32[]{:S(2)}) async-start(f32[32,1,128]{2,1,0:T(1,128)} %bitcast.11), calls=%async_computation | async-start | bytes 32768 | tf_op jit(solution)/shard_map/all_to_all | solution.py:71
  116.0 1.2 scatter_custom_fusion.2
  117.3 4.9 %all-to-all-done = f32[32,1,128]{2,1,0:T(1,128)S(1)} async-done(((f32[32,1,128]{2,1,0:T(1,128)}), f32[32,1,128]{2,1,0:T(1,128)S(1)}, u32[]{:S(2)}, u32[]{:S(2)}) %all-to-all-start) | async-done | bytes 16416 | tf_op jit(solution)/shard_map/all_to_all | solution.py:71
  122.2 4.9 %all-to-all-start.2 = ((f32[32,1,128]{2,1,0:T(1,128)}), f32[32,1,128]{2,1,0:T(1,128)S(1)}, u32[]{:S(2)}, u32[]{:S(2)}) async-start(f32[32,1,128]{2,1,0:T(1,128)} %bitcast.22), calls=%async_computation.2 | async-start | bytes 32768 | tf_op jit(solution)/shard_map/all_to_all | solution.py:85
  127.2 6.1 %all-to-all-done.2 = f32[32,1,128]{2,1,0:T(1,128)S(1)} async-done(((f32[32,1,128]{2,1,0:T(1,128)}), f32[32,1,128]{2,1,0:T(1,128)S(1)}, u32[]{:S(2)}, u32[]{:S(2)}) %all-to-all-start.2) | async-done | bytes 16416 | tf_op jit(solution)/shard_map/all_to_all | solution.py:85
  133.4 0.6 subtract_bitcast_fusion
  134.0 0.6 gather_fusion.3
  134.6 0.7 bitcast_select_fusion
  135.3 4.9 %all-to-all-start.3 = ((f32[32,1,128]{2,1,0:T(1,128)}), f32[32,1,128]{2,1,0:T(1,128)S(1)}, u32[]{:S(2)}, u32[]{:S(2)}) async-start(f32[32,1,128]{2,1,0:T(1,128)} %bitcast.29), calls=%async_computation.3 | async-start | bytes 32768 | tf_op jit(solution)/shard_map/all_to_all | solution.py:101
  140.2 0.2 reduce-scatter.5.cloned.1.call-start
  140.5 5.9 %all-to-all-done.3 = f32[32,1,128]{2,1,0:T(1,128)S(1)} async-done(((f32[32,1,128]{2,1,0:T(1,128)}), f32[32,1,128]{2,1,0:T(1,128)S(1)}, u32[]{:S(2)}, u32[]{:S(2)}) %all-to-all-start.3) | async-done | bytes 16416 | tf_op jit(solution)/shard_map/all_to_all | solution.py:101
  146.4 0.6 gather_fusion.4
  146.9 10.5 %select_convert_fusion = bf16[1024,4096]{1,0:T(8,128)(2,1)S(1)} fusion(f32[1024,4096]{1,0:T(8,128)} %copy-done, f32[1024]{0:T(1024)S(1)} %bitcast.109, s32[1024]{0:T(1024)S(1)} %add_select_fusion.1, pred[1024]{0:T(1024)(128)(4,1)S(1)} %broadcast_bitcast_fusion, pred[1024]{0:T(1024)(128)(4,1)S(1)} %fusion.14), kind=kLoop, calls=%fused_computation.9 | loop fusion | flops 29360128 | bytes 25176064 | tf_op jit(solution)/shard_map/convert_element_type | solution.py:108
  157.4 3.2 copy-done.1
  160.6 8.9 %convolution_convert_fusion = bf16[4096,768]{1,0:T(8,128)(2,1)} fusion(bf16[1024,4096]{1,0:T(8,128)(2,1)S(1)} %select_convert_fusion, bf16[1024,768]{1,0:T(8,128)(2,1)S(1)} %bitcast.99), kind=kOutput, calls=%fused_computation.14 | convolution fusion | flops 6445596672 | bytes 16252928 | tf_op jit(solution)/shard_map/dot_general | solution.py:127
  169.6 10.9 %fusion.5 = bf16[1024,768]{1,0:T(8,128)(2,1)S(1)} fusion(bf16[1024,4096]{1,0:T(8,128)(2,1)} %copy-done.1, bf16[1,4096,768]{2,1,0:T(8,128)(2,1)} %param.6), kind=kOutput, calls=%fused_computation.19 | convolution fusion | flops 6443237376 | bytes 16252928 | tf_op jit(solution)/shard_map/dot_general | solution.py:110
  180.5 0.2 broadcast_select_fusion
  180.7 6.1 %broadcast_in_dim.235 = bf16[64,128,768]{2,1,0:T(8,128)(2,1)} broadcast(bf16[]{:T(256)} %constant.59.clone.1), dimensions={} | broadcast | bytes 12582914 | tf_op jit(solution)/shard_map/broadcast_in_dim | solution.py:116
  186.8 7.2 %scatter_fusion = bf16[64,128,768]{2,1,0:T(8,128)(2,1)} fusion(bf16[64,128,768]{2,1,0:T(8,128)(2,1)} %broadcast_in_dim.235, s32[8]{0:T(128)S(1)} %fusion.30, bf16[8,128,768]{2,1,0:T(8,128)(2,1)S(1)} %broadcast_select_fusion), kind=kCustom, calls=%fused_computation.8 | custom fusion | flops 786432 | bytes 4718624 | tf_op jit(solution)/shard_map/scatter-add | solution.py:118
  194.1 38.1 %reduce-scatter.5.cloned.1.call-done = bf16[1024,768]{1,0:T(8,128)(2,1)} async-done(((bf16[4096,768]{1,0:T(8,128)(2,1)}), bf16[1024,768]{1,0:T(8,128)(2,1)}) %reduce-scatter.5.cloned.1.call-update) | async-done | bytes 1572880 | tf_op jit(solution)/shard_map/reduce_scatter | solution.py:126
  232.1 3.3 bitcast_convert_fusion
  235.4 104.5 %reduce-scatter.3.cloned.1.call-done = bf16[256,768]{1,0:T(8,128)(2,1)} async-done(((bf16[8192,768]{1,0:T(8,128)(2,1)}), bf16[256,768]{1,0:T(8,128)(2,1)}) %reduce-scatter.3.cloned.1.call-update) | async-done | bytes 393232 | tf_op jit(solution)/shard_map/reduce_scatter | solution.py:120
  339.9 1.9 convert_element_type.40
  (24 shorter events, 0.8 us)
Async XLA Ops:
  7.2 68.6 %all-gather.4.cloned.1.call-start = ((), (), s32[]{:S(2)}) async-start(), calls=%async_computation.6 | async-start | bytes 12976128 | tf_op jit(solution)/shard_map/all_gather | solution.py:49
  90.0 8.0 %copy-start = (f32[1024,4096]{1,0:T(8,128)}, f32[1024,4096]{1,0:T(8,128)S(1)}, u32[]{:S(2)}) copy-start(f32[1024,4096]{1,0:T(8,128)S(1)} %get-tuple-element.12) | copy-start | bytes 50331652
  99.3 11.8 %all-to-all-start.1 = ((f32[32,1,128]{2,1,0:T(1,128)}), f32[32,1,128]{2,1,0:T(1,128)S(1)}, u32[]{:S(2)}, u32[]{:S(2)}) async-start(f32[32,1,128]{2,1,0:T(1,128)} %bitcast.15), calls=%async_computation.1 | async-start | bytes 32768 | tf_op jit(solution)/shard_map/all_to_all | solution.py:78
  111.1 11.1 %all-to-all-start = ((f32[32,1,128]{2,1,0:T(1,128)}), f32[32,1,128]{2,1,0:T(1,128)S(1)}, u32[]{:S(2)}, u32[]{:S(2)}) async-start(f32[32,1,128]{2,1,0:T(1,128)} %bitcast.11), calls=%async_computation | async-start | bytes 32768 | tf_op jit(solution)/shard_map/all_to_all | solution.py:71
  122.2 11.1 %all-to-all-start.2 = ((f32[32,1,128]{2,1,0:T(1,128)}), f32[32,1,128]{2,1,0:T(1,128)S(1)}, u32[]{:S(2)}, u32[]{:S(2)}) async-start(f32[32,1,128]{2,1,0:T(1,128)} %bitcast.22), calls=%async_computation.2 | async-start | bytes 32768 | tf_op jit(solution)/shard_map/all_to_all | solution.py:85
  135.3 11.1 %all-to-all-start.3 = ((f32[32,1,128]{2,1,0:T(1,128)}), f32[32,1,128]{2,1,0:T(1,128)S(1)}, u32[]{:S(2)}, u32[]{:S(2)}) async-start(f32[32,1,128]{2,1,0:T(1,128)} %bitcast.29), calls=%async_computation.3 | async-start | bytes 32768 | tf_op jit(solution)/shard_map/all_to_all | solution.py:101
  140.2 91.9 %reduce-scatter.5.cloned.1.call-start = ((), (), s32[]{:S(2)}) async-start(), calls=%async_computation.8 | async-start | bytes 7864320 | tf_op jit(solution)/shard_map/reduce_scatter | solution.py:126
  157.4 3.2 copy-start.1
  169.6 170.3 %reduce-scatter.3.cloned.1.call-start = ((), (), s32[]{:S(2)}) async-start(), calls=%async_computation.7 | async-start | bytes 12976128 | tf_op jit(solution)/shard_map/reduce_scatter | solution.py:120
Sparse Core Ops, SparseCore 0:
  10.3 65.4 all-gather.3
  169.7 62.3 reduce-scatter.4
  235.9 103.9 reduce-scatter.2
where the time goes:
time: 349 us; the launch traced here: 348 us
  waiting for transfers between devices  178 us (51%)
  blocking collectives  47.1 us (13%)
  other arithmetic  42.6 us (12%)
  matrix products  28.8 us (8%)
  starting transfers between devices  20.8 us (6%)
  local copies, waits for them, and re-layouts  17.2 us (5%)
  between operations  13.9 us (4%)
    reduce_scatter x1, waiting for transfers between devices, per_device(): lax.psum_scatter(dense.reshape(label_size * home_blocks * block_rows, fea...  104 us
    reduce_scatter x1, waiting for transfers between devices, per_device(): lax.psum_scatter(lax.dot_general(slope, flat_rows, (((0,), (0,)), ((), ()...  38.1 us
    all_gather x1, blocking collectives, per_device(): lax.all_gather(beam, 'label', axis=0, tiled=True)  25.2 us
    all_gather x1, blocking collectives, per_device(): lax.all_gather(positives, 'label', axis=0, tiled=True)  21.9 us
    all_gather x1, waiting for transfers between devices, per_device(): everyone = lax.all_gather(queries, 'label', axis=0, tiled=True)  12.9 us
    dot_general x1, matrix products, per_device(): jnp.dot(slope, ranker, preferred_element_type=jnp.float32)  10.9 us
    convert_element_type x1, other arithmetic, per_device(): slope = jnp.where(active_rows[:, None], jnp.exp(scores - normal_rows[:, N...  10.5 us
    dot_general x1, matrix products, per_device(): lax.dot_general(flat_rows, ranker, (((1,), (1,)), ((), ())), preferred_el...  8.98 us
  transfers between devices with their start and end apart: 7, of which 7 were waited for; matrix products, arithmetic and copies ran while one was open for 11% of the time, Pallas kernels for 0%

commit v1 on v0

v1 whole, which is shorter than its diff:
```python
import functools

import jax
import jax.numpy as jnp
from jax import lax
from jax.experimental import pallas as pl
from jax.experimental.pallas import tpu as pltpu
from jax.sharding import PartitionSpec as P

F32 = jnp.float32
BF16 = jnp.bfloat16
NDEV = 32
SLOTS = 8
ROWS = 128
FEAT = 768
HALF = 384
LABELS = 4096
TILE = 512
NEG = -1e30
BIG = 1e30


def iota(shape, dim):
    return lax.broadcasted_iota(jnp.int32, shape, dim)


def dot(a, b, dims):
    return lax.dot_general(a, b, (dims, ((), ())), preferred_element_type=F32)


def ones_where(mask):
    return jnp.where(mask, 1.0, 0.0).astype(BF16)


def slot_table(meta, held):
    n = held.shape[0]
    r = iota((256, 64), 0)
    q = iota((256, 64), 1)
    pick = ones_where((r // 8 == q % 32) & (r % 8 == 6 + q // 32))
    beams = dot(meta, pick, ((0,), (0,)))
    hit = held == beams[0:1, :]
    for k in range(1, 4):
        hit = hit | (held == beams[k : k + 1, :])
    hit = hit & (iota((n, 64), 1) >= 0)
    before = ones_where(iota((64, 64), 0) < iota((64, 64), 1))
    rank = dot(ones_where(hit), before, ((1,), (0,)))
    slot = (iota((n, 64), 0) % SLOTS).astype(F32)
    return jnp.where(hit & (rank == slot), 1.0, 0.0)


def piece_matrix(table):
    e = iota((64, 512), 1)
    spread = ones_where(iota((64, 512), 0) == e // 8)
    wide = dot(table.astype(BF16), spread, ((1,), (0,)))
    full = jnp.broadcast_to(wide[:, None, :], (256, 8, 512))
    same = iota((256, 8, 512), 1) == iota((256, 8, 512), 2) % 8
    return jnp.where(same, full, 0.0).reshape(2048, 512).astype(BF16)


def route_kernel(got_ref, held_ref, out_ref):
    got = got_ref[...]
    table = slot_table(got[:, FEAT:], held_ref[...][:, :1])
    m = piece_matrix(table)
    out = dot(m[:, :256], got[:, :HALF], ((1,), (0,)))
    out += dot(m[:, 256:], got[:, HALF:FEAT], ((1,), (0,)))
    out_ref[...] = out.astype(BF16)


def table_kernel(got_ref, held_ref, mine_ref, sel_ref, mask_ref, col_ref):
    meta = got_ref[...][:, FEAT:]
    table = slot_table(meta, held_ref[...][:, :1])
    sel_ref[...] = piece_matrix(table)
    mine = mine_ref[...]
    own = slot_table(meta, mine[:, 0:1])
    row = iota((16, 64), 0)
    q = iota((16, 64), 1).astype(F32)
    home = jnp.where(q == (row.astype(F32) - 8.0) * 32.0 + mine[:, 1:2], 1.0, 0.0)
    own = jnp.where(row < 8, own, jnp.where(row < 10, home, 0.0)).astype(BF16)
    mask = dot(table.astype(BF16), own, ((1,), (1,)))
    mask_ref[...] = jnp.concatenate([mask, jnp.zeros((256, 112), F32)], axis=1)
    qq = iota((64, 256), 0)
    rr = iota((64, 256), 1)
    part = []
    for c in range(3):
        pick = ones_where((rr // 8 == qq % 32) & (rr % 8 == 3 * (qq // 32) + c))
        where_c = dot(own, pick, ((1,), (0,))).astype(BF16)
        part.append(dot(where_c, meta, ((1,), (0,))))
    inside = part[0] == mine[:, 0:1] + 1.0
    col = jnp.where(inside, part[1] * 64.0 + part[2], -1.0).astype(jnp.int32)
    for s in range(SLOTS):
        col_ref[:, s * ROWS : (s + 1) * ROWS] = jnp.broadcast_to(col[s : s + 1, :], (8, ROWS))


def scores_kernel(q_ref, w_ref, s_ref, lse_ref, top, total):
    step = pl.program_id(0)

    @pl.when(step == 0)
    def _():
        top[...] = jnp.full_like(top, NEG)
        total[...] = jnp.zeros_like(total)

    sub = 256
    for i in range(TILE // sub):
        s = dot(w_ref[i * sub : (i + 1) * sub, :], q_ref[...], ((1,), (1,)))
        s_ref[i * sub : (i + 1) * sub, :] = s
        blocks = s.reshape(sub // 8, 8, s.shape[1])
        old = top[...]
        new = jnp.maximum(old, jnp.max(blocks, axis=0))
        total[...] = total[...] * jnp.exp(old - new) + jnp.sum(jnp.exp(blocks - new[None]), axis=0)
        top[...] = new

    @pl.when(step == pl.num_programs(0) - 1)
    def _():
        m = top[...]
        high = jnp.max(m, axis=0, keepdims=True)
        tot = jnp.sum(total[...] * jnp.exp(m - high), axis=0, keepdims=True)
        lse = high + jnp.log(tot)
        for s in range(SLOTS):
            piece = lse[:, s * ROWS : (s + 1) * ROWS]
            lse_ref[:, s : s + 1, :] = jnp.broadcast_to(piece[None], (NDEV, 1, ROWS))


def normal_kernel(lse_ref, mask_ref, norm_ref, home_ref):
    lse = lse_ref[...]
    mask = mask_ref[...]
    for s in range(SLOTS + 2):
        use = mask[:, s : s + 1] > 0.5
        kept = jnp.where(use, lse, NEG)
        high = jnp.max(kept, axis=0, keepdims=True)
        tot = jnp.sum(jnp.where(use, jnp.exp(kept - high), 0.0), axis=0, keepdims=True)
        value = jnp.where(high > 0.5 * NEG, high + jnp.log(tot), BIG)
        if s < SLOTS:
            norm_ref[:, s * ROWS : (s + 1) * ROWS] = jnp.broadcast_to(value, (8, ROWS))
        else:
            home_ref[s - SLOTS : s - SLOTS + 1, :] = value


def slope_of(s, norm_ref, col_ref, first):
    target = iota(s.shape, 0) + first == col_ref[0:1, :]
    return jnp.exp(s - norm_ref[0:1, :]) - jnp.where(target, 1.0, 0.0), target


def table_grad_kernel(tiles_ref, q_ref, s_ref, norm_ref, col_ref, *out_refs):
    step = pl.program_id(0)
    slope, _ = slope_of(s_ref[...], norm_ref, col_ref, tiles_ref[step] * TILE)
    value = dot(slope.astype(BF16), q_ref[...], ((1,), (0,)))
    for i, ref in enumerate(out_refs):

        @pl.when(step == i)
        def _(ref=ref):
            ref[...] = value.astype(ref.dtype)


def query_grad_kernel(w_ref, s_ref, norm_ref, col_ref, part_ref, pick_ref, acc, pick):
    step = pl.program_id(0)

    @pl.when(step == 0)
    def _():
        acc[...] = jnp.zeros_like(acc)
        pick[...] = jnp.zeros_like(pick)

    s = s_ref[...]
    slope, target = slope_of(s, norm_ref, col_ref, step * TILE)
    found = jnp.where(target, s, 0.0)
    pick[...] += jnp.sum(found.reshape(TILE // 8, 8, s.shape[1]), axis=0)
    acc[...] += dot(slope.astype(BF16), w_ref[...], ((0,), (0,)))

    @pl.when(step == pl.num_programs(0) - 1)
    def _():
        part_ref[...] = acc[...].astype(BF16)
        chosen = jnp.sum(pick[...], axis=0, keepdims=True)
        for s in range(SLOTS):
            piece = chosen[:, s * ROWS : (s + 1) * ROWS]
            pick_ref[:, s : s + 1, :] = jnp.broadcast_to(piece[None], (NDEV, 1, ROWS))


def params(limit=48):
    return pltpu.CompilerParams(vmem_limit_bytes=limit << 20)


def whole(kernel, out_shape, *args):
    return pl.pallas_call(kernel, out_shape=out_shape, compiler_params=params())(*args)


def shape(dims, dtype):
    return jax.ShapeDtypeStruct(dims, dtype)


def fixed(dims):
    return pl.BlockSpec(dims, lambda *_: (0,) * len(dims))


def table_grads(tiles, q, s, norm, col, dtypes):
    n = len(dtypes)
    rows = q.shape[0]
    spec = pltpu.PrefetchScalarGridSpec(
        num_scalar_prefetch=1,
        grid=(n,),
        in_specs=[
            fixed((rows, FEAT)),
            pl.BlockSpec((TILE, rows), lambda i, t: (t[i], 0)),
            fixed((8, rows)),
            fixed((8, rows)),
        ],
        out_specs=[fixed((TILE, FEAT)) for _ in dtypes],
    )
    return pl.pallas_call(
        table_grad_kernel,
        grid_spec=spec,
        out_shape=[shape((TILE, FEAT), d) for d in dtypes],
        compiler_params=params(),
        cost_estimate=pl.CostEstimate(
            flops=2 * n * TILE * rows * FEAT,
            transcendentals=n * TILE * rows,
            bytes_accessed=n * TILE * rows * 4 + rows * FEAT * 2,
        ),
    )(tiles, q, s, norm, col)


def per_device(queries, weights, beam, positives, owner):
    me = lax.axis_index("label")
    y = lax.axis_index("dp")
    rows = SLOTS * ROWS
    ranker = weights[0]

    def swap(x):
        return lax.all_to_all(x, "label", split_axis=0, concat_axis=0, tiled=True)

    ids = jnp.arange(NDEV, dtype=jnp.int32)
    held = jnp.sum(jnp.where(owner[None, :] == ids[:, None], ids[None, :], 0), axis=1).astype(F32)
    held_rows = jnp.broadcast_to(held[:, None, None], (NDEV, SLOTS, 128)).reshape(256, 128)
    my_block = jnp.sum(jnp.where(owner == me, ids, 0)).astype(F32)
    mine = jnp.where(iota((16, 128), 1) == 0, my_block, me.astype(F32))

    low = positives & (LABELS - 1)
    coded = jnp.stack([(positives >> 12) + 1, low >> 6, low & 63], axis=0).reshape(3, 2, ROWS)
    coded = coded.transpose(1, 0, 2).reshape(6, ROWS)
    wide_beam = jnp.pad(beam, ((0, 0), (0, ROWS - beam.shape[1])), constant_values=-1)
    meta = jnp.concatenate([coded, wide_beam], axis=0).astype(BF16)
    pieces = queries.reshape(2, 16, 8, 2, HALF).transpose(1, 3, 2, 0, 4).reshape(NDEV, 8, FEAT)
    pieces = jnp.concatenate([pieces, jnp.broadcast_to(meta[None], (NDEV, 8, ROWS))], axis=2)
    got = swap(pieces).reshape(256, FEAT + ROWS)

    sent = whole(route_kernel, shape((2048, HALF), BF16), got, held_rows)
    arrived = swap(sent.reshape(NDEV, 64, HALF))
    sel, mask, col = whole(
        table_kernel,
        (shape((2048, 512), BF16), shape((256, 128), F32), shape((8, rows), jnp.int32)),
        got,
        held_rows,
        mine,
    )
    q = arrived.reshape(16, 2, SLOTS, 8, HALF).transpose(2, 0, 3, 1, 4).reshape(rows, FEAT)

    steps = LABELS // TILE
    scores, lse = pl.pallas_call(
        scores_kernel,
        grid=(steps,),
        in_specs=[fixed((rows, FEAT)), pl.BlockSpec((TILE, FEAT), lambda i: (i, 0))],
        out_specs=[pl.BlockSpec((TILE, rows), lambda i: (i, 0)), fixed((NDEV, SLOTS, ROWS))],
        out_shape=[shape((LABELS, rows), F32), shape((NDEV, SLOTS, ROWS), F32)],
        scratch_shapes=[pltpu.VMEM((8, rows), F32), pltpu.VMEM((8, rows), F32)],
        compiler_params=params(),
        cost_estimate=pl.CostEstimate(
            flops=2 * LABELS * rows * FEAT,
            transcendentals=LABELS * rows,
            bytes_accessed=LABELS * rows * 4 + LABELS * FEAT * 2,
        ),
    )(q, ranker)
    all_lse = swap(lse).reshape(256, ROWS)
    norm, home_norm = whole(
        normal_kernel, (shape((8, rows), F32), shape((2, ROWS), F32)), all_lse, mask
    )

    up = [(i, (i + 1) % 4) for i in range(4)]
    down = [(i, (i + 3) % 4) for i in range(4)]
    across, ahead, behind = (y + 2) % 4 * 2, (y + 1) % 4 * 2, (y + 3) % 4 * 2
    own = y * 2

    def tiles(*names):
        return jnp.stack(names).astype(jnp.int32)

    far_a, far_b = table_grads(tiles(across, across + 1), q, scores, norm, col, (BF16, BF16))
    via_up = lax.ppermute(far_a, "dp", up)
    via_down = lax.ppermute(far_b, "dp", down)
    next_b, prev_a = table_grads(tiles(ahead + 1, behind), q, scores, norm, col, (BF16, BF16))
    from_prev_b = lax.ppermute(next_b, "dp", up)
    from_next_a = lax.ppermute(prev_a, "dp", down)
    next_a, prev_b, own_a, own_b = table_grads(
        tiles(ahead, behind + 1, own, own + 1), q, scores, norm, col, (F32, F32, F32, F32)
    )
    norm_late, next_a, prev_b, own_a, own_b = lax.optimization_barrier(
        (norm, next_a, prev_b, own_a, own_b)
    )

    part, picked = pl.pallas_call(
        query_grad_kernel,
        grid=(steps,),
        in_specs=[
            pl.BlockSpec((TILE, FEAT), lambda i: (i, 0)),
            pl.BlockSpec((TILE, rows), lambda i: (i, 0)),
            fixed((8, rows)),
            fixed((8, rows)),
        ],
        out_specs=[fixed((rows, FEAT)), fixed((NDEV, SLOTS, ROWS))],
        out_shape=[shape((rows, FEAT), BF16), shape((NDEV, SLOTS, ROWS), F32)],
        scratch_shapes=[pltpu.VMEM((rows, FEAT), F32), pltpu.VMEM((8, rows), F32)],
        compiler_params=params(),
        cost_estimate=pl.CostEstimate(
            flops=2 * LABELS * rows * FEAT,
            transcendentals=LABELS * rows,
            bytes_accessed=LABELS * rows * 4 + LABELS * FEAT * 2,
        ),
    )(ranker, scores, norm_late, col)
    back = part.reshape(SLOTS, 16, 8, 2, HALF).transpose(1, 3, 0, 2, 4).reshape(NDEV, 64, HALF)
    parts = swap(back).reshape(2048, HALF)
    summed = dot(sel, parts, ((0,), (0,))).astype(BF16)
    homeward = summed.reshape(2, NDEV, 8, HALF).transpose(1, 2, 0, 3).reshape(NDEV, 8, FEAT)
    home = swap(homeward).reshape(16, 2, 8, 2, HALF)
    grad_queries = home.transpose(3, 0, 2, 1, 4).reshape(256, FEAT).astype(F32)

    all_picked = swap(picked).reshape(256, ROWS)
    home_mask = mask[:, SLOTS : SLOTS + 2]
    positive = jnp.sum(home_mask[:, :, None] * all_picked[:, None, :], axis=0)
    loss = (home_norm - positive).reshape(-1)

    relay_up = (next_a + via_up.astype(F32)).astype(BF16)
    relay_down = (prev_b + via_down.astype(F32)).astype(BF16)
    from_prev_a = lax.ppermute(relay_up, "dp", up)
    from_next_b = lax.ppermute(relay_down, "dp", down)
    grad_a = own_a + from_prev_a.astype(F32) + from_next_a.astype(F32)
    grad_b = own_b + from_prev_b.astype(F32) + from_next_b.astype(F32)
    grad_table = jnp.concatenate([grad_a, grad_b], axis=0)
    return loss, grad_queries, grad_table[None]


def solution(mesh):
    placed = (
        P(("dp", "label"), None),
        P("label", None, None),
        P(("dp", "label"), None),
        P(("dp", "label")),
        P(),
    )
    return jax.shard_map(
        per_device,
        mesh=mesh,
        in_specs=placed,
        out_specs=(P(("dp", "label")), P(("dp", "label"), None), P("label", "dp", None)),
        check_vma=False,
    )
```

time: 349 us -> 194 us (0.56)
  waiting for transfers between devices: 178 us -> 54.9 us
  Pallas kernels: 0 us -> 56.1 us
  blocking collectives: 47.1 us -> 0 us
  other arithmetic: 42.6 us -> 13.3 us
  starting transfers between devices: 20.8 us -> 48.4 us
  matrix products: 28.8 us -> 2.68 us
  between operations: 13.9 us -> 1.59 us
    reduce_scatter x2 -> x0, waiting for transfers between devices: 143 us -> none  [the longest x1 104 us: per_device(): lax.psum_scatter(dense.reshape(label_size * home_blocks * block_rows, fea...]
    pallas_call x0 -> x8, Pallas kernels: none -> 56.1 us  [the longest x3 20.6 us: table_grads(): pl.pallas_call(table_grad_kernel, grid_spec=spec, out_shape=[shape((TILE,...]
    all_gather x2 -> x0, blocking collectives: 47.1 us -> none  [the longest x1 25.2 us: per_device(): lax.all_gather(beam, 'label', axis=0, tiled=True)]
    dot_general x3 -> x1, matrix products: 28.8 us -> 2.68 us  [dot(): return lax.dot_general(a, b, (dims, ((), ())), preferred_element_type=F32)]
    ppermute x0 -> x6, waiting for transfers between devices: none -> 20.6 us  [the longest x1 10.6 us: per_device(): from_prev_a = lax.ppermute(relay_up, 'dp', up)]
    all_to_all x4 -> x6, starting transfers between devices: 20.5 us -> 39.7 us  [swap(): return lax.all_to_all(x, 'label', split_axis=0, concat_axis=0, tiled=True)]
    all_gather x1 -> x0, waiting for transfers between devices: 12.9 us -> none  [per_device(): everyone = lax.all_gather(queries, 'label', axis=0, tiled=True)]
    all_to_all x4 -> x6, waiting for transfers between devices: 21.7 us -> 34.3 us  [swap(): return lax.all_to_all(x, 'label', split_axis=0, concat_axis=0, tiled=True)]
  transfers between devices with their start and end apart: 7 -> 12, of which waited for: 7 -> 6; matrix products, arithmetic and copies ran while one was open for 11% -> 10% of each run, Pallas kernels for 0% -> 7%
where the time goes in v1:
time: 194 us; the launch traced here: 192 us
  Pallas kernels  56.1 us (29%)
  waiting for transfers between devices  54.9 us (28%)
  starting transfers between devices  48.4 us (25%)
  local copies, waits for them, and re-layouts  15.1 us (8%)
  other arithmetic  13.3 us (7%)
  matrix products  2.68 us (1%)
    all_to_all x6, starting transfers between devices, swap(): return lax.all_to_all(x, 'label', split_axis=0, concat_axis=0, tiled=True)  39.7 us
    all_to_all x6, waiting for transfers between devices, swap(): return lax.all_to_all(x, 'label', split_axis=0, concat_axis=0, tiled=True)  34.3 us
    pallas_call x3, Pallas kernels, table_grads(): pl.pallas_call(table_grad_kernel, grid_spec=spec, out_shape=[shape((TILE,...  20.6 us
    pallas_call x1, Pallas kernels, per_device(): pl.pallas_call(query_grad_kernel, grid=(steps,), in_specs=[pl.BlockSpec((...  16.4 us
    pallas_call x1, Pallas kernels, per_device(): pl.pallas_call(scores_kernel, grid=(steps,), in_specs=[fixed((rows, FEAT)...  14.4 us
    ppermute x1, waiting for transfers between devices, per_device(): from_prev_a = lax.ppermute(relay_up, 'dp', up)  10.6 us
    unnamed x27, local copies, waits for them, and re-layouts  6.69 us
    ppermute x1, waiting for transfers between devices, per_device(): via_down = lax.ppermute(far_b, 'dp', down)  6.57 us
  transfers between devices with their start and end apart: 12, of which 6 were waited for; matrix products, arithmetic and copies ran while one was open for 10% of the time, Pallas kernels for 7%

profile of v1, /device:TPU:2, one launch (start us, length us, event | category | flops | bytes accessed | tf_op | source)
XLA Modules:
  0.0 192.0 jit_solution(8579697706737565949)
XLA Ops:
  0.6 0.7 fusion.2
  1.4 0.7 convert.26
  2.0 1.0 copy.20
  3.1 0.8 pad_maximum_fusion
  3.9 8.5 %all-to-all-start = ((bf16[32,8,896]{2,1,0:T(8,128)(2,1)}), bf16[32,8,896]{2,1,0:T(8,128)(2,1)S(1)}, u32[]{:S(2)}, u32[]{:S(2)}) async-start(bf16[32,8,896]{2,1,0:T(8,128)(2,1)} %pad_maximum_fusion), calls=%async_computation | async-start | bytes 917504 | tf_op jit(solution)/shard_map/all_to_all | solution.py:227
  12.7 9.5 %all-to-all-done = bf16[32,8,896]{2,1,0:T(8,128)(2,1)S(1)} async-done(((bf16[32,8,896]{2,1,0:T(8,128)(2,1)}), bf16[32,8,896]{2,1,0:T(8,128)(2,1)S(1)}, u32[]{:S(2)}, u32[]{:S(2)}) %all-to-all-start) | async-done | bytes 458784 | tf_op jit(solution)/shard_map/all_to_all | solution.py:227
  22.3 2.9 %shard_map.76 = bf16[2048,384]{1,0:T(8,128)(2,1)} custom-call(bf16[256,896]{1,0:T(8,128)(2,1)S(1)} %bitcast.52, f32[256,128]{1,0:T(8,128)S(1)} %broadcast_in_dim.52.held_ref), custom_call_target="tpu_custom_call" | custom-call | tf_op jit(solution)/shard_map/pallas_call | solution.py:182
  25.2 5.7 %all-to-all-start.1 = ((bf16[32,64,384]{2,1,0:T(8,128)(2,1)}), bf16[32,64,384]{2,1,0:T(8,128)(2,1)}, u32[]{:S(2)}, u32[]{:S(2)}) async-start(bf16[32,64,384]{2,1,0:T(8,128)(2,1)} %bitcast.8), calls=%async_computation.1 | async-start | bytes 3145728 | tf_op jit(solution)/shard_map/all_to_all | solution.py:227
  30.9 0.6 fusion.5
  32.3 20.8 %all-to-all-done.1 = bf16[32,64,384]{2,1,0:T(8,128)(2,1)} async-done(((bf16[32,64,384]{2,1,0:T(8,128)(2,1)}), bf16[32,64,384]{2,1,0:T(8,128)(2,1)}, u32[]{:S(2)}, u32[]{:S(2)}) %all-to-all-start.1) | async-done | bytes 1572896 | tf_op jit(solution)/shard_map/all_to_all | solution.py:227
  53.1 1.6 copy.22
  54.7 14.4 %shard_map.77 = (f32[4096,1024]{1,0:T(8,128)}, f32[32,8,128]{2,1,0:T(8,128)}) custom-call(bf16[1024,768]{1,0:T(8,128)(2,1)S(1)} %bitcast.48, bf16[4096,768]{1,0:T(8,128)(2,1)} %bitcast.65), custom_call_target="tpu_custom_call" | custom-call | flops 6442450944 | bytes 23068672 | tf_op jit(solution)/shard_map/pallas_call | solution.py:256
  69.1 5.6 %all-to-all-start.2 = ((f32[32,8,128]{2,1,0:T(8,128)}), f32[32,8,128]{2,1,0:T(8,128)S(1)}, u32[]{:S(2)}, u32[]{:S(2)}) async-start(f32[32,8,128]{2,1,0:T(8,128)} %get-tuple-element.25), calls=%async_computation.2 | async-start | bytes 262144 | tf_op jit(solution)/shard_map/all_to_all | solution.py:227
  74.9 1.3 shard_map.78
  76.2 1.3 copy-done.2
  77.5 4.0 %all-to-all-done.2 = f32[32,8,128]{2,1,0:T(8,128)S(1)} async-done(((f32[32,8,128]{2,1,0:T(8,128)}), f32[32,8,128]{2,1,0:T(8,128)S(1)}, u32[]{:S(2)}, u32[]{:S(2)}) %all-to-all-start.2) | async-done | bytes 131104 | tf_op jit(solution)/shard_map/all_to_all | solution.py:227
  81.5 0.5 shard_map.79
  82.0 9.3 %shard_map.80 = (f32[512,768]{1,0:T(8,128)S(1)}, f32[512,768]{1,0:T(8,128)S(1)}, f32[512,768]{1,0:T(8,128)S(1)}, f32[512,768]{1,0:T(8,128)}) custom-call(s32[4]{0:T(128)S(1)} %pad_add_fusion.tiles_ref, bf16[1024,768]{1,0:T(8,128)(2,1)} %bitcast.49, f32[4096,1024]{1,0:T(8,128)} %get-tuple-element.28.s_ref, f32[8,1024]{1,0:T(8,128)S(1)} %get-tuple-element.35.norm_ref, ...), custom_call_target="tpu_custom_call" | custom-call | flops 3221225472 | bytes 9961472 | tf_op jit(solution)/shard_map/pallas_call | solution.py:207
  91.3 1.2 copy-done.4
  92.5 1.1 copy-done.8
  93.6 16.4 %shard_map.81 = (bf16[1024,768]{1,0:T(8,128)(2,1)S(1)}, f32[32,8,128]{2,1,0:T(8,128)}) custom-call(bf16[4096,768]{1,0:T(8,128)(2,1)} %bitcast.66, f32[4096,1024]{1,0:T(8,128)} %get-tuple-element.28.s_ref, f32[8,1024]{1,0:T(8,128)S(1)} %get-tuple-element.35.norm_ref, s32[8,1024]{1,0:T(8,128)S(1)} %get-tuple-element.30.col_ref), custom_call_target="tpu_custom_call" | custom-call | flops 6442450944 | bytes 23068672 | tf_op jit(solution)/shard_map/pallas_call | solution.py:296
  110.0 1.2 copy-done.6
  111.2 4.9 %all-to-all-start.3 = ((f32[32,8,128]{2,1,0:T(8,128)}), f32[32,8,128]{2,1,0:T(8,128)S(1)}, u32[]{:S(2)}, u32[]{:S(2)}) async-start(f32[32,8,128]{2,1,0:T(8,128)} %get-tuple-element.36), calls=%async_computation.3 | async-start | bytes 262144 | tf_op jit(solution)/shard_map/all_to_all | solution.py:227
  116.1 5.5 %shard_map.82 = (bf16[512,768]{1,0:T(8,128)(2,1)}, bf16[512,768]{1,0:T(8,128)(2,1)S(1)}) custom-call(s32[2]{0:T(128)S(1)} %pad_add_fusion.1.tiles_ref, bf16[1024,768]{1,0:T(8,128)(2,1)S(1)} %bitcast.50, f32[4096,1024]{1,0:T(8,128)} %get-tuple-element.28.s_ref, f32[8,1024]{1,0:T(8,128)S(1)} %get-tuple-element.35.norm_ref, s32[8,1024]{1,0:T(8,128)S(1)} %get-tuple-element.30.col_ref), custom_call_target="tpu_custom_call" | custom-call | flops 1610612736 | bytes 5767168 | tf_op jit(solution)/shard_map/pallas_call | solution.py:207
  121.6 0.9 copy-done.10
  122.5 1.6 collective-permute-start
  124.1 1.5 copy.24
  125.6 7.5 %all-to-all-start.4 = ((bf16[32,64,384]{2,1,0:T(8,128)(2,1)}), bf16[32,64,384]{2,1,0:T(8,128)(2,1)}, u32[]{:S(2)}, u32[]{:S(2)}) async-start(bf16[32,64,384]{2,1,0:T(8,128)(2,1)} %bitcast.56), calls=%async_computation.4 | async-start | bytes 3145728 | tf_op jit(solution)/shard_map/all_to_all | solution.py:227
  133.2 1.9 collective-permute-start.4
  135.1 0.8 slice.3
  135.9 1.0 copy.23
  136.9 5.8 %shard_map.83 = (bf16[512,768]{1,0:T(8,128)(2,1)}, bf16[512,768]{1,0:T(8,128)(2,1)}) custom-call(s32[2]{0:T(128)S(1)} %pad_add_fusion.2.tiles_ref, bf16[1024,768]{1,0:T(8,128)(2,1)S(1)} %bitcast.51, f32[4096,1024]{1,0:T(8,128)} %get-tuple-element.28.s_ref, f32[8,1024]{1,0:T(8,128)S(1)} %get-tuple-element.35.norm_ref, s32[8,1024]{1,0:T(8,128)S(1)} %get-tuple-element.30.col_ref), custom_call_target="tpu_custom_call" | custom-call | flops 1610612736 | bytes 5767168 | tf_op jit(solution)/shard_map/pallas_call | solution.py:207
  142.7 1.8 collective-permute-start.2
  144.9 2.3 %add_convert_fusion.1 = bf16[512,768]{1,0:T(8,128)(2,1)} fusion(f32[512,768]{1,0:T(8,128)S(1)} %get-tuple-element.40, bf16[512,768]{1,0:T(8,128)(2,1)} %collective-permute-done), kind=kLoop, calls=%fused_computation.4 | loop fusion | flops 1179648 | bytes 3145728 | tf_op jit(solution)/shard_map/convert_element_type | solution.py:327
  147.5 6.6 %collective-permute-done.4 = bf16[512,768]{1,0:T(8,128)(2,1)} collective-permute-done((bf16[512,768]{1,0:T(8,128)(2,1)}, bf16[512,768]{1,0:T(8,128)(2,1)}, u32[]{:S(2)}, u32[]{:S(2)}) %collective-permute-start.4) | collective-permute-done | bytes 786464 | tf_op jit(solution)/shard_map/ppermute | solution.py:285
  154.1 2.2 %add_convert_fusion = bf16[512,768]{1,0:T(8,128)(2,1)} fusion(f32[512,768]{1,0:T(8,128)S(1)} %copy-done.5, bf16[512,768]{1,0:T(8,128)(2,1)} %collective-permute-done.4), kind=kLoop, calls=%fused_computation.2 | loop fusion | flops 1179648 | bytes 3145728 | tf_op jit(solution)/shard_map/convert_element_type | solution.py:328
  156.3 2.9 %collective-permute-start.5 = (bf16[512,768]{1,0:T(8,128)(2,1)}, bf16[512,768]{1,0:T(8,128)(2,1)S(1)}, u32[]{:S(2)}, u32[]{:S(2)}) collective-permute-start(bf16[512,768]{1,0:T(8,128)(2,1)} %add_convert_fusion), channel_id=1, source_target_pairs={{0,96},{32,0},{64,32},{96,64},{1,97},{33,1},{65,33},{97,65},{2,98}... | collective-permute-start | bytes 2359304 | tf_op jit(solution)/shard_map/ppermute | solution.py:330
  159.2 0.6 subtract_bitcast_fusion
  159.8 2.7 %convolution_convert_fusion = bf16[512,384]{1,0:T(8,128)(2,1)S(1)} fusion(bf16[2048,512]{1,0:T(8,128)(2,1)S(1)} %copy-done.3, bf16[2048,384]{1,0:T(8,128)(2,1)} %bitcast.23), kind=kOutput, calls=%fused_computation.5 | convolution fusion | flops 805502976 | bytes 4063232 | tf_op jit(solution)/shard_map/dot_general | solution.py:28
  162.9 1.0 reshape.99
  163.9 7.4 %all-to-all-start.5 = ((bf16[32,8,768]{2,1,0:T(8,128)(2,1)}), bf16[32,8,768]{2,1,0:T(8,128)(2,1)S(1)}, u32[]{:S(2)}, u32[]{:S(2)}) async-start(bf16[32,8,768]{2,1,0:T(8,128)(2,1)} %reshape.99), calls=%async_computation.5 | async-start | bytes 786432 | tf_op jit(solution)/shard_map/all_to_all | solution.py:227
  171.3 10.6 %collective-permute-done.1 = bf16[512,768]{1,0:T(8,128)(2,1)} collective-permute-done((bf16[512,768]{1,0:T(8,128)(2,1)}, bf16[512,768]{1,0:T(8,128)(2,1)}, u32[]{:S(2)}, u32[]{:S(2)}) %collective-permute-start.1) | collective-permute-done | bytes 786464 | tf_op jit(solution)/shard_map/ppermute | solution.py:329
  181.9 1.6 convert_add_fusion.1
  183.5 3.4 %collective-permute-done.5 = bf16[512,768]{1,0:T(8,128)(2,1)S(1)} collective-permute-done((bf16[512,768]{1,0:T(8,128)(2,1)}, bf16[512,768]{1,0:T(8,128)(2,1)S(1)}, u32[]{:S(2)}, u32[]{:S(2)}) %collective-permute-start.5) | collective-permute-done | bytes 786464 | tf_op jit(solution)/shard_map/ppermute | solution.py:330
  186.9 1.4 convert_add_fusion
  188.3 1.9 maximum_bitcast_fusion
  190.2 0.4 reshape.101
  191.0 0.9 copy.27
  (47 shorter events, 2.3 us)
Async XLA Ops:
  0.6 11.8 %copy-start.12 = (s32[32]{0:T(128)S(1)}, s32[32]{0:T(128)}, u32[]{:S(2)}) copy-start(s32[32]{0:T(128)} %param.9) | copy-start | bytes 388
  3.9 18.3 %all-to-all-start = ((bf16[32,8,896]{2,1,0:T(8,128)(2,1)}), bf16[32,8,896]{2,1,0:T(8,128)(2,1)S(1)}, u32[]{:S(2)}, u32[]{:S(2)}) async-start(bf16[32,8,896]{2,1,0:T(8,128)(2,1)} %pad_maximum_fusion), calls=%async_computation | async-start | bytes 917504 | tf_op jit(solution)/shard_map/all_to_all | solution.py:227
  25.2 28.0 %all-to-all-start.1 = ((bf16[32,64,384]{2,1,0:T(8,128)(2,1)}), bf16[32,64,384]{2,1,0:T(8,128)(2,1)}, u32[]{:S(2)}, u32[]{:S(2)}) async-start(bf16[32,64,384]{2,1,0:T(8,128)(2,1)} %bitcast.8), calls=%async_computation.1 | async-start | bytes 3145728 | tf_op jit(solution)/shard_map/all_to_all | solution.py:227
  54.7 14.4 %copy-start = (bf16[8,16,8,2,384]{4,2,3,1,0:T(8,128)(2,1)}, bf16[8,16,8,2,384]{4,2,3,1,0:T(8,128)(2,1)S(1)}, u32[]{:S(2)}) copy-start(bf16[8,16,8,2,384]{4,2,3,1,0:T(8,128)(2,1)S(1)} %copy.22) | copy-start | bytes 4718596
  69.1 12.4 %all-to-all-start.2 = ((f32[32,8,128]{2,1,0:T(8,128)}), f32[32,8,128]{2,1,0:T(8,128)S(1)}, u32[]{:S(2)}, u32[]{:S(2)}) async-start(f32[32,8,128]{2,1,0:T(8,128)} %get-tuple-element.25), calls=%async_computation.2 | async-start | bytes 262144 | tf_op jit(solution)/shard_map/all_to_all | solution.py:227
  76.2 1.3 copy-start.2
  91.3 1.2 copy-start.4
  92.5 1.1 copy-start.8
  93.6 22.5 %copy-start.1 = (bf16[8,16,8,2,384]{4,2,3,1,0:T(8,128)(2,1)S(1)}, bf16[8,16,8,2,384]{4,2,3,1,0:T(8,128)(2,1)}, u32[]{:S(2)}) copy-start(bf16[8,16,8,2,384]{4,2,3,1,0:T(8,128)(2,1)} %copy-done) | copy-start | bytes 4718596
  110.0 1.2 copy-start.6
  111.2 14.4 %all-to-all-start.3 = ((f32[32,8,128]{2,1,0:T(8,128)}), f32[32,8,128]{2,1,0:T(8,128)S(1)}, u32[]{:S(2)}, u32[]{:S(2)}) async-start(f32[32,8,128]{2,1,0:T(8,128)} %get-tuple-element.36), calls=%async_computation.3 | async-start | bytes 262144 | tf_op jit(solution)/shard_map/all_to_all | solution.py:227
  116.1 8.0 %copy-start.7 = (bf16[1024,768]{1,0:T(8,128)(2,1)S(1)}, bf16[1024,768]{1,0:T(8,128)(2,1)}, u32[]{:S(2)}) copy-start(bf16[1024,768]{1,0:T(8,128)(2,1)} %copy-done.6) | copy-start | bytes 4718596
  121.6 0.9 copy-start.10
  122.5 22.3 %collective-permute-start = (bf16[512,768]{1,0:T(8,128)(2,1)}, bf16[512,768]{1,0:T(8,128)(2,1)}, u32[]{:S(2)}, u32[]{:S(2)}) collective-permute-start(bf16[512,768]{1,0:T(8,128)(2,1)} %get-tuple-element.41), channel_id=1, source_target_pairs={{0,32},{32,64},{64,96},{96,0},{1,33},{33,65},{65,97},{97,1},{2,34}... | collective-permute-start | bytes 2359304 | tf_op jit(solution)/shard_map/ppermute | solution.py:284
  125.6 34.2 %all-to-all-start.4 = ((bf16[32,64,384]{2,1,0:T(8,128)(2,1)}), bf16[32,64,384]{2,1,0:T(8,128)(2,1)}, u32[]{:S(2)}, u32[]{:S(2)}) async-start(bf16[32,64,384]{2,1,0:T(8,128)(2,1)} %bitcast.56), calls=%async_computation.4 | async-start | bytes 3145728 | tf_op jit(solution)/shard_map/all_to_all | solution.py:227
  133.2 21.0 %collective-permute-start.4 = (bf16[512,768]{1,0:T(8,128)(2,1)}, bf16[512,768]{1,0:T(8,128)(2,1)}, u32[]{:S(2)}, u32[]{:S(2)}) collective-permute-start(bf16[512,768]{1,0:T(8,128)(2,1)} %copy-done.10), channel_id=1, source_target_pairs={{0,96},{32,0},{64,32},{96,64},{1,97},{33,1},{65,33},{97,65},{2,98}... | collective-permute-start | bytes 2359304 | tf_op jit(solution)/shard_map/ppermute | solution.py:285
  142.7 28.6 %collective-permute-start.2 = (bf16[512,768]{1,0:T(8,128)(2,1)}, bf16[512,768]{1,0:T(8,128)(2,1)}, u32[]{:S(2)}, u32[]{:S(2)}) collective-permute-start(bf16[512,768]{1,0:T(8,128)(2,1)} %get-tuple-element.42), channel_id=1, source_target_pairs={{0,96},{32,0},{64,32},{96,64},{1,97},{33,1},{65,33},{97,65},{2,98}... | collective-permute-start | bytes 2359304 | tf_op jit(solution)/shard_map/ppermute | solution.py:288
  144.5 39.0 %collective-permute-start.3 = (bf16[512,768]{1,0:T(8,128)(2,1)}, bf16[512,768]{1,0:T(8,128)(2,1)}, u32[]{:S(2)}, u32[]{:S(2)}) collective-permute-start(bf16[512,768]{1,0:T(8,128)(2,1)} %get-tuple-element.44), channel_id=1, source_target_pairs={{0,32},{32,64},{64,96},{96,0},{1,33},{33,65},{65,97},{97,1},{2,34}... | collective-permute-start | bytes 2359304 | tf_op jit(solution)/shard_map/ppermute | solution.py:287
  144.8 9.3 %copy-start.5 = (f32[512,768]{1,0:T(8,128)S(1)}, f32[512,768]{1,0:T(8,128)}, u32[]{:S(2)}) copy-start(f32[512,768]{1,0:T(8,128)} %copy-done.4) | copy-start | bytes 4718596
  147.2 12.6 %copy-start.3 = (bf16[2048,512]{1,0:T(8,128)(2,1)S(1)}, bf16[2048,512]{1,0:T(8,128)(2,1)}, u32[]{:S(2)}) copy-start(bf16[2048,512]{1,0:T(8,128)(2,1)} %copy-done.2) | copy-start | bytes 6291460
  147.2 34.7 %collective-permute-start.1 = (bf16[512,768]{1,0:T(8,128)(2,1)}, bf16[512,768]{1,0:T(8,128)(2,1)}, u32[]{:S(2)}, u32[]{:S(2)}) collective-permute-start(bf16[512,768]{1,0:T(8,128)(2,1)} %add_convert_fusion.1), channel_id=1, source_target_pairs={{0,32},{32,64},{64,96},{96,0},{1,33},{33,65},{65,97},{97,1},{2,34}... | collective-permute-start | bytes 2359304 | tf_op jit(solution)/shard_map/ppermute | solution.py:329
  156.3 30.6 %collective-permute-start.5 = (bf16[512,768]{1,0:T(8,128)(2,1)}, bf16[512,768]{1,0:T(8,128)(2,1)S(1)}, u32[]{:S(2)}, u32[]{:S(2)}) collective-permute-start(bf16[512,768]{1,0:T(8,128)(2,1)} %add_convert_fusion), channel_id=1, source_target_pairs={{0,96},{32,0},{64,32},{96,64},{1,97},{33,1},{65,33},{97,65},{2,98}... | collective-permute-start | bytes 2359304 | tf_op jit(solution)/shard_map/ppermute | solution.py:330
  162.5 19.4 %copy-start.9 = (f32[512,768]{1,0:T(8,128)S(1)}, f32[512,768]{1,0:T(8,128)}, u32[]{:S(2)}) copy-start(f32[512,768]{1,0:T(8,128)} %copy-done.8) | copy-start | bytes 4718596
  163.9 26.3 %all-to-all-start.5 = ((bf16[32,8,768]{2,1,0:T(8,128)(2,1)}), bf16[32,8,768]{2,1,0:T(8,128)(2,1)S(1)}, u32[]{:S(2)}, u32[]{:S(2)}) async-start(bf16[32,8,768]{2,1,0:T(8,128)(2,1)} %reshape.99), calls=%async_computation.5 | async-start | bytes 786432 | tf_op jit(solution)/shard_map/all_to_all | solution.py:227
  171.3 15.6 %copy-start.11 = (f32[512,768]{1,0:T(8,128)S(1)}, f32[512,768]{1,0:T(8,128)}, u32[]{:S(2)}) copy-start(f32[512,768]{1,0:T(8,128)} %get-tuple-element.43) | copy-start | bytes 4718596
